TPU v7x, 256 devices: a whole 4x4x8 slice. The times are simulated.
256 devices in a mesh: section: 4 (over y_hi, core), dp: 64 (over x, y_lo, z).
Axes of the slice: x: 4, y: 4 (y_hi: 2, y_lo: 2; y = y_hi * 2 + y_lo), z: 8, core: 2. Of those that a mesh axis runs over, the one named last changes fastest.
Arguments:
- activations: bfloat16 [4, 16384, 8192], P('section', 'dp'), may hold values from -600 to 600, as said below
- tail_grads: bfloat16 [4, 16384, 512], P('section', 'dp'), may hold values from -48 to 48, as said below
- tail_slots: int32 [4, 64, 4], P('section', 'dp'), may hold values from 0 to 3, each once within a row
- master: float32 [4, 8192, 512], P('section', 'dp'), may hold values from -6 to 6
- moment1: float32 [4, 8192, 512], P('section', 'dp'), may hold values from -0.00029296876 to 0.00029296876
- moment2: float32 [4, 8192, 512], P('section', 'dp'), may hold values from 1.1920929e-09 to 2.9802322e-08
- overflow: int32 [4, 64], P('section', 'dp'), may hold values from 0 to 1, as said below
- clip_on: int32 [4], P('section'), may hold values from 0 to 1, as said below
- next_inputs: bfloat16 [4, 2048, 8192], P('section', 'dp'), may hold values from -6 to 6
Outputs:
- new_master: float32 [4, 8192, 512], P('section', 'dp')
- next_out: bfloat16 [4, 2048, 512], P('section', 'dp')
Inputs may be any that keep to these rules, and one draw needn't show every extreme that they name: `tail_slots`: each row along the last dimension names every slot once. `overflow`: at least one shard is flagged and at least one is not. `clip_on`: at least one section is clipped and at least one is not. `activations`: real-valued. `tail_grads`: real-valued.
All inputs are finite; a program needn't handle non-finite values.
Results may differ from a plain program's by a relative error of at most 0.0049.
Values may be sent and summed in bfloat16 or wider, within the bound.
No kernel may reach another device: no remote copies, remote signals or barrier semaphores. Data moves between devices by JAX's collectives and lax.ppermute only.
A program may use at most 64 MiB of HBM per device.

v0:
```python
import functools
import math

import jax
import jax.numpy as jnp
from jax import lax
from jax.experimental import pallas as pl
from jax.experimental.pallas import tpu as pltpu
from jax.sharding import Mesh
from jax.sharding import PartitionSpec as P

DP = ("x", "y_lo", "z")
YZ = ("y_lo", "z")
SECTION = ("y_hi", "core")
EVERY = SECTION + DP

NX, NY, NZ = 4, 2, 8
TAILS = 4
COUNT = 4 * NX * NY * NZ


beta_one = 0.9
beta_two = 0.95
correct_one = 1.0 - 0.9**20
correct_two = 1.0 - 0.95**20
adam_eps = 1e-08
decay_rate = 0.1
learn_rate = 0.1

f32 = jnp.float32
bf16 = jnp.bfloat16

ROWS = 128
COLS = 512
HALF = COLS // 2
Z_WIDE = NX * ROWS


def column(x, y, z):
    return pl.multiple_of((x * (NY * NZ) + y * NZ + z) * ROWS, ROWS)


def side_columns(where, side, away, acts, turn=0):
    owner = lax.rem(where[1] + away, NZ)
    xs = [lax.rem(turn + k, NX) for k in range(NX)]
    return jnp.concatenate([acts[:, pl.ds(column(x, side, owner), ROWS)] for x in xs], axis=1)


def partner_pairs(joined):
    tail = joined[joined.shape[1] // 2 :, :]
    half = tail.shape[1] // 2
    return jnp.concatenate([tail[:, :half], tail[:, half:]], axis=0)


def z_terms(where, away, rows, pairs, acts, joined, part):
    own = jnp.dot(
        pairs[rows, :], side_columns(where, where[2], away, acts), preferred_element_type=f32
    )
    term = own + jnp.dot(partner_pairs(joined)[rows, :], part, preferred_element_type=f32)
    for k in range(NX):
        yield k, term[:, k * ROWS : (k + 1) * ROWS]


HALVES = slice(0, HALF), slice(HALF, COLS)


def first_kernel(where, tails, *refs):
    acts, (pairs, give, placed) = refs[:NX], refs[NX:]
    tail = tails.shape[0] // TAILS

    def place(t, carry):
        src = pl.ds(pl.multiple_of(t * tail, tail), tail)
        dst = pl.ds(pl.multiple_of(where[3 + t] * tail, tail), tail)
        placed[dst, :] = tails[src, :]
        return carry

    lax.fori_loop(0, TAILS, place, 0)
    tokens = tails.shape[0]
    value = placed[...].astype(f32).T.astype(bf16)
    pairs[...] = value
    for k in range(NX):
        give[:tokens, k * ROWS : (k + 1) * ROWS] = acts[k][...]
    give[tokens:, :tokens] = value[:HALF]
    give[tokens:, tokens:] = value[HALF:]


def pack_kernel(where, acts, *gives):
    for k, give in enumerate(gives):
        away = NZ // 2 - 1 - k
        for n, far in enumerate((away, NZ - away) if away else (0,)):
            give[:, n * Z_WIDE : (n + 1) * Z_WIDE] = side_columns(where, 1 - where[2], far, acts)


def first_z_kernel(where, pairs, acts, joined, out_p, out_m):
    part = joined[: acts.shape[0], :]
    for k, term in z_terms(where, NZ // 2, slice(0, COLS), pairs, acts, joined, part):
        out_p[k] = term[:HALF].astype(bf16)
        out_m[k] = term[HALF:].astype(bf16)


def later_z_kernel(s, half, ways, where, pairs, acts, joined, part, *refs):
    came, outs = dict(zip(ways, refs)), refs[len(ways) :]
    away = NZ // 2 - s
    for way, far in enumerate((away, NZ - away)):
        columns = slice(way * Z_WIDE, (way + 1) * Z_WIDE)
        for k, term in z_terms(where, far, HALVES[half], pairs, acts, joined, part[:, columns]):
            if way in came:
                term = term + came[way][k].astype(f32)
            outs[way][k] = term.astype(bf16)


def own_z_kernel(where, pairs, acts, joined, part, out):
    mine = jnp.dot(
        pairs[...], side_columns(where, where[2], 0, acts, where[0]), preferred_element_type=f32
    )
    xs = [lax.rem(where[0] + r, NX) for r in range(NX)]
    parts = [part[:, pl.ds(pl.multiple_of(x * ROWS, ROWS), ROWS)] for x in xs]
    out[...] = mine + jnp.dot(
        partner_pairs(joined), jnp.concatenate(parts, axis=1), preferred_element_type=f32
    )


def last_z_kernel(where, term, *refs):
    gots, own, sends = refs[:4], refs[4], refs[5:]
    for r in range(NX):
        x = lax.rem(where[0] + r, NX)
        for half, rows in enumerate(HALVES):
            up, down = gots[2 * half : 2 * half + 2]
            total = term[rows, r * ROWS : (r + 1) * ROWS] + up[x].astype(f32) + down[x].astype(f32)
            if r == 0:
                own[rows, :] = total
            else:
                sends[r - 1][rows, :] = total.astype(bf16)


def gradient_kernel(scale, overflow, own, *refs):
    gots, (grad, squares) = refs[: NX - 1], refs[NX - 1 :]
    total = own[...]
    for got in gots:
        total += got[...].astype(f32)
    total = total.T * scale
    grad[...] = total
    kept = jnp.where(overflow[0, 0] == 0, 1.0, 0.0)
    squares[...] = jnp.broadcast_to(jnp.sum(total * total) * kept, squares.shape)


def adam_kernel(overflow, clip_on, squares, grad, old_master, old_one, old_two, *refs):
    gots, states, (master, weights) = refs[: NX - 1], refs[NX - 1 : 2 * NX - 2], refs[2 * NX - 2 :]
    norm = jnp.sqrt(jnp.sum(squares[...], axis=0, keepdims=True))
    factor = jnp.where(clip_on[0] == 1, 1.0 / jnp.maximum(norm, 1.0), 1.0)
    own_keep = jnp.where(overflow[0, 0] == 0, 1.0, 0.0)
    for r in range(NX):
        for c in range(COLS // ROWS):
            lanes = slice(c * ROWS, (c + 1) * ROWS)
            if r == 0:
                old, one, two = (ref[:, lanes] for ref in (old_master, old_one, old_two))
                gradient = grad[:, lanes]
                keep = jnp.broadcast_to(own_keep, (1, ROWS))
            else:
                state = states[r - 1]
                old, one, two = (state[k * ROWS : (k + 1) * ROWS, lanes] for k in range(3))
                gradient = gots[r - 1][:, lanes].astype(f32)
                keep = state[3 * ROWS : 3 * ROWS + 1, lanes]
            clipped = gradient * factor
            m_next = beta_one * one + (1.0 - beta_one) * clipped
            v_next = beta_two * two + (1.0 - beta_two) * (clipped * clipped)
            update = (
                m_next / correct_one / (jnp.sqrt(v_next / correct_two) + adam_eps)
                + decay_rate * old
            )
            new = jnp.where(keep > 0.5, old - learn_rate * update, old)
            if r == 0:
                master[:, lanes] = new
            weights[r * ROWS : (r + 1) * ROWS, lanes] = new.astype(bf16)


def tokens_kernel(where, mine, out):
    for r in range(NX):
        owner = lax.rem(where[0] + r, NX)
        for g in range(NY * NZ):
            start = pl.multiple_of((owner * (NY * NZ) + g) * ROWS, ROWS)
            out[g, :, r * ROWS : (r + 1) * ROWS] = mine[:, pl.ds(start, ROWS)]


def near(x):
    return pltpu.with_memory_space_constraint(x, pltpu.VMEM)


def far(x):
    return pltpu.with_memory_space_constraint(x, pltpu.HBM)


SCALARS = pl.BlockSpec(memory_space=pltpu.SMEM)
GRANT = pltpu.CompilerParams(vmem_limit_bytes=8 * 2**20)
NEAR = pl.BlockSpec(memory_space=pltpu.VMEM)


def on_core(kernel, scalars, arrays, outs, scratch=(), place=near, grant=GRANT):
    return pl.pallas_call(
        kernel,
        in_specs=[SCALARS] * len(scalars) + [NEAR] * len(arrays),
        out_specs=[NEAR] * len(outs),
        out_shape=list(outs),
        scratch_shapes=scratch,
        compiler_params=grant,
    )(*scalars, *[place(a) for a in arrays])


def shift(x, axis, n, by):
    return lax.ppermute(x, axis, [(i, (i + by) % n) for i in range(n)])


def swap_side(x):
    return shift(x, "y_lo", NY, 1)


def first_terms(where, tails, acts):
    tokens = tails.shape[0]
    block = lambda x: lambda i, w: (
        0,
        x * (NY * NZ) + (1 - w[2]) * NZ + lax.rem(w[1] + NZ // 2, NZ),
    )
    whole = lambda *shape: pl.BlockSpec(shape, lambda i, w: (0, 0))
    shapes = (COLS, tokens), (2 * tokens, Z_WIDE)
    return pl.pallas_call(
        first_kernel,
        grid_spec=pltpu.PrefetchScalarGridSpec(
            num_scalar_prefetch=1,
            grid=(1,),
            in_specs=[whole(*tails.shape)]
            + [pl.BlockSpec((tokens, ROWS), block(x)) for x in range(NX)],
            out_specs=[whole(*shape) for shape in shapes],
            scratch_shapes=[pltpu.VMEM(tails.shape, bf16)],
        ),
        out_shape=[jax.ShapeDtypeStruct(shape, bf16) for shape in shapes],
        compiler_params=GRANT,
        name="work_first",
    )(where, far(tails), *([far(acts)] * NX))


def sum_terms(where, tails, acts):
    tokens = acts.shape[0]
    two = lambda *shape: [pltpu.VMEM(shape, bf16)] * 2
    z_pairs, give = first_terms(where, tails, acts)
    wide = [2 * Z_WIDE] * (NZ // 2 - 1) + [Z_WIDE]
    gives = on_core(pack_kernel, [where], [acts], [pltpu.VMEM((tokens, w), bf16) for w in wide])
    joined, *parts = [swap_side(g) for g in [give, *gives]]

    up, down = on_core(first_z_kernel, [where], [z_pairs, acts, joined], two(NX, HALF, ROWS))
    gots = {(0, 0): shift(up, "z", NZ, 1), (1, 1): shift(down, "z", NZ, -1)}
    for s in range(1, NZ // 2):
        came, gots = gots, {}
        for half in range(2):
            ways = [way for way in range(2) if (half, way) in came]
            up, down = on_core(
                functools.partial(later_z_kernel, s, half, ways),
                [where],
                [z_pairs, acts, joined, parts[s - 1], *[came[half, way] for way in ways]],
                two(NX, HALF, ROWS),
            )
            gots[half, 0] = shift(up, "z", NZ, 1)
            gots[half, 1] = shift(down, "z", NZ, -1)
    gots = [gots[half, way] for half in range(2) for way in range(2)]
    piece = lambda t: pltpu.VMEM((COLS, ROWS), t)
    (term,) = on_core(
        own_z_kernel, [where], [z_pairs, acts, joined, parts[-1]], [pltpu.VMEM((COLS, Z_WIDE), f32)]
    )
    own, *sends = on_core(
        last_z_kernel, [where], [term, *gots], [piece(f32)] + [piece(bf16)] * (NX - 1)
    )
    gots = [shift(send, "x", NX, r + 1) for r, send in enumerate(sends)]
    return own, gots


def local(
    activations, tail_grads, tail_slots, master, moment1, moment2, overflow, clip_on, next_inputs
):
    acts = activations[0]
    tails = tail_grads[0]
    tok_dev, width = acts.shape
    toks = next_inputs.shape[1]
    where = jnp.stack([lax.axis_index(a) for a in ("x", "z", "y_lo")]).astype(jnp.int32)
    where = jnp.concatenate([where, tail_slots[0, 0]])

    tokens = jax.ShapeDtypeStruct((NY * NZ, toks, NX * ROWS), bf16)
    (tokens,) = on_core(tokens_kernel, [where], [next_inputs[0]], [tokens])
    tokens = lax.all_to_all(tokens, YZ, 0, 0, tiled=True)

    keep = jnp.where(overflow[0, 0] == 0, 1.0, 0.0)
    state = [master[0], moment1[0], moment2[0], jnp.full((8, COLS), keep, f32)]
    state = jnp.concatenate(state, axis=0)
    states = [shift(state, "x", NX, -r) for r in range(1, NX)]

    own, gots = sum_terms(where, tails, acts)
    gradient, part_sq = on_core(
        functools.partial(gradient_kernel, 1.0 / (tok_dev * NX * NY * NZ)),
        [overflow],
        [own, *gots],
        [pltpu.VMEM((ROWS, COLS), f32), pltpu.VMEM((1, ROWS), f32)],
    )
    part_sq = jnp.broadcast_to(part_sq[None], (COUNT, 1, ROWS))
    squares = lax.all_to_all(part_sq, EVERY, 0, 0, tiled=True).reshape(COUNT, ROWS)
    gots = [shift(gradient.astype(bf16), "x", NX, -r) for r in range(1, NX)]
    updated, along_x = on_core(
        adam_kernel,
        [overflow, clip_on],
        [squares, gradient, master[0], moment1[0], moment2[0], *gots, *states],
        [
            jax.ShapeDtypeStruct((ROWS, COLS), f32),
            jax.ShapeDtypeStruct((NX * ROWS, COLS), bf16),
        ],
        place=lambda a: a,
        grant=pltpu.CompilerParams(vmem_limit_bytes=12 * 2**20),
    )
    partial = jnp.einsum("gtk,kc->gtc", tokens, along_x, preferred_element_type=f32).astype(bf16)
    parts = lax.all_to_all(partial, YZ, 0, 0, tiled=True)
    result = jnp.sum(parts.astype(f32), axis=0)
    next_out = (result * (1.0 / math.sqrt(width))).astype(bf16)
    return (updated[None], next_out[None])


def solution(mesh):
    finer = Mesh(mesh.devices.reshape(2, 2, NX, NY, NZ), EVERY)
    return jax.shard_map(
        local,
        mesh=finer,
        in_specs=(
            P(SECTION, DP, None),
            P(SECTION, DP, None),
            P(SECTION, DP, None),
            P(SECTION, DP, None),
            P(SECTION, DP, None),
            P(SECTION, DP, None),
            P(SECTION, DP),
            P(SECTION),
            P(SECTION, DP, None),
        ),
        out_specs=(P(SECTION, DP, None), P(SECTION, DP, None)),
        check_vma=False,
    )
```

profile of v0, /device:TPU:1, one launch (start us, length us, event | category | flops | bytes accessed | tf_op | source)
XLA Modules:
  0.0 181.9 jit_solution(4693318627237076347)
XLA Ops:
  1.4 2.0 %work_first.1 = (bf16[512,256]{1,0:T(8,128)(2,1)S(1)}, bf16[512,512]{1,0:T(8,128)(2,1)S(1)}) custom-call(s32[7]{0:T(128)S(1)} %pad_add_fusion.where, bf16[256,512]{1,0:T(8,128)(2,1)} %bitcast.42, bf16[256,8192]{1,0:T(8,128)(2,1)} %bitcast.20, bf16[256,8192]{1,0:T(8,128)(2,1)} %bitcast.21, bf16[256,8192]{1,0:T(8,128)(2,1)} %bitcast.22, bf16[256,8192]{1,0:T(8,128)(2,1)} %bitcast.23), custom_call_target="tpu_custom_call" | custom-call | tf_op jit(solution)/shard_map/work_first/pallas_call | solution.py:225
  3.4 2.2 %collective-permute-start = (bf16[512,512]{1,0:T(8,128)(2,1)S(1)}, bf16[512,512]{1,0:T(8,128)(2,1)S(1)}, u32[]{:S(2)}, u32[]{:S(2)}) collective-permute-start(bf16[512,512]{1,0:T(8,128)(2,1)S(1)} %get-tuple-element.31), channel_id=1, source_target_pairs={{0,8},{8,0},{1,9},{9,1},{2,10},{10,2},{3,11},{11,3},{4,12},{12,4},... | collective-permute-start | bytes 1572872 | tf_op jit(solution)/shard_map/ppermute | solution.py:210
  8.2 7.8 %collective-permute-done.joined = bf16[512,512]{1,0:T(8,128)(2,1)S(1)} collective-permute-done((bf16[512,512]{1,0:T(8,128)(2,1)S(1)}, bf16[512,512]{1,0:T(8,128)(2,1)S(1)}, u32[]{:S(2)}, u32[]{:S(2)}) %collective-permute-start) | collective-permute-done | bytes 524320 | tf_op jit(solution)/shard_map/ppermute | solution.py:210
  17.0 6.7 %collective-permute-start.12 = (bf16[4,256,128]{2,1,0:T(8,128)(2,1)S(1)}, bf16[4,256,128]{2,1,0:T(8,128)(2,1)S(1)}, u32[]{:S(2)}, u32[]{:S(2)}) collective-permute-start(bf16[4,256,128]{2,1,0:T(8,128)(2,1)S(1)} %get-tuple-element.43), channel_id=1, source_target_pairs={{0,7},{1,0},{2,1},{3,2},{4,3},{5,4},{6,5},{7,6},{8,15},{9,8},{10,9... | collective-permute-start | bytes 786440 | tf_op jit(solution)/shard_map/ppermute | solution.py:210
  25.0 2.3 %collective-permute-done.4.part = bf16[256,1024]{1,0:T(8,128)(2,1)S(1)} collective-permute-done((bf16[256,1024]{1,0:T(8,128)(2,1)S(1)}, bf16[256,1024]{1,0:T(8,128)(2,1)S(1)}, u32[]{:S(2)}, u32[]{:S(2)}) %collective-permute-start.4) | collective-permute-done | bytes 524320 | tf_op jit(solution)/shard_map/ppermute | solution.py:210
  28.3 2.8 %collective-permute-start.13 = (bf16[4,256,128]{2,1,0:T(8,128)(2,1)S(1)}, bf16[4,256,128]{2,1,0:T(8,128)(2,1)S(1)}, u32[]{:S(2)}, u32[]{:S(2)}) collective-permute-start(bf16[4,256,128]{2,1,0:T(8,128)(2,1)S(1)} %get-tuple-element.44), channel_id=1, source_target_pairs={{0,1},{1,2},{2,3},{3,4},{4,5},{5,6},{6,7},{7,0},{8,9},{9,10},{10,1... | collective-permute-start | bytes 786440 | tf_op jit(solution)/shard_map/ppermute | solution.py:210
  31.1 4.0 %collective-permute-start.14 = (bf16[4,256,128]{2,1,0:T(8,128)(2,1)S(1)}, bf16[4,256,128]{2,1,0:T(8,128)(2,1)S(1)}, u32[]{:S(2)}, u32[]{:S(2)}) collective-permute-start(bf16[4,256,128]{2,1,0:T(8,128)(2,1)S(1)} %get-tuple-element.45), channel_id=1, source_target_pairs={{0,7},{1,0},{2,1},{3,2},{4,3},{5,4},{6,5},{7,6},{8,15},{9,8},{10,9... | collective-permute-start | bytes 786440 | tf_op jit(solution)/shard_map/ppermute | solution.py:210
  36.2 2.3 %collective-permute-done.3.part = bf16[256,1024]{1,0:T(8,128)(2,1)S(1)} collective-permute-done((bf16[256,1024]{1,0:T(8,128)(2,1)S(1)}, bf16[256,1024]{1,0:T(8,128)(2,1)S(1)}, u32[]{:S(2)}, u32[]{:S(2)}) %collective-permute-start.3) | collective-permute-done | bytes 524320 | tf_op jit(solution)/shard_map/ppermute | solution.py:210
  38.5 6.6 %collective-permute-start.7 = (bf16[4,256,128]{2,1,0:T(8,128)(2,1)S(1)}, bf16[4,256,128]{2,1,0:T(8,128)(2,1)S(1)}, u32[]{:S(2)}, u32[]{:S(2)}) collective-permute-start(bf16[4,256,128]{2,1,0:T(8,128)(2,1)S(1)} %get-tuple-element.38), channel_id=1, source_target_pairs={{0,7},{1,0},{2,1},{3,2},{4,3},{5,4},{6,5},{7,6},{8,15},{9,8},{10,9... | collective-permute-start | bytes 786440 | tf_op jit(solution)/shard_map/ppermute | solution.py:210
  46.2 2.7 %collective-permute-start.16 = (bf16[4,256,128]{2,1,0:T(8,128)(2,1)S(1)}, bf16[4,256,128]{2,1,0:T(8,128)(2,1)S(1)}, u32[]{:S(2)}, u32[]{:S(2)}) collective-permute-start(bf16[4,256,128]{2,1,0:T(8,128)(2,1)S(1)} %get-tuple-element.47), channel_id=1, source_target_pairs={{0,7},{1,0},{2,1},{3,2},{4,3},{5,4},{6,5},{7,6},{8,15},{9,8},{10,9... | collective-permute-start | bytes 786440 | tf_op jit(solution)/shard_map/ppermute | solution.py:210
  50.0 2.9 %collective-permute-start.9 = (bf16[4,256,128]{2,1,0:T(8,128)(2,1)S(1)}, bf16[4,256,128]{2,1,0:T(8,128)(2,1)S(1)}, u32[]{:S(2)}, u32[]{:S(2)}) collective-permute-start(bf16[4,256,128]{2,1,0:T(8,128)(2,1)S(1)} %get-tuple-element.40), channel_id=1, source_target_pairs={{0,7},{1,0},{2,1},{3,2},{4,3},{5,4},{6,5},{7,6},{8,15},{9,8},{10,9... | collective-permute-start | bytes 786440 | tf_op jit(solution)/shard_map/ppermute | solution.py:210
  56.1 3.5 %collective-permute-start.18 = (bf16[4,256,128]{2,1,0:T(8,128)(2,1)S(1)}, bf16[4,256,128]{2,1,0:T(8,128)(2,1)S(1)}, u32[]{:S(2)}, u32[]{:S(2)}) collective-permute-start(bf16[4,256,128]{2,1,0:T(8,128)(2,1)S(1)} %get-tuple-element.49), channel_id=1, source_target_pairs={{0,7},{1,0},{2,1},{3,2},{4,3},{5,4},{6,5},{7,6},{8,15},{9,8},{10,9... | collective-permute-start | bytes 786440 | tf_op jit(solution)/shard_map/ppermute | solution.py:210
  61.1 3.6 %collective-permute-start.11 = (bf16[4,256,128]{2,1,0:T(8,128)(2,1)S(1)}, bf16[4,256,128]{2,1,0:T(8,128)(2,1)S(1)}, u32[]{:S(2)}, u32[]{:S(2)}) collective-permute-start(bf16[4,256,128]{2,1,0:T(8,128)(2,1)S(1)} %get-tuple-element.42), channel_id=1, source_target_pairs={{0,7},{1,0},{2,1},{3,2},{4,3},{5,4},{6,5},{7,6},{8,15},{9,8},{10,9... | collective-permute-start | bytes 786440 | tf_op jit(solution)/shard_map/ppermute | solution.py:210
  65.8 5.3 %collective-permute-done.10.refs_0_ = bf16[4,256,128]{2,1,0:T(8,128)(2,1)S(1)} collective-permute-done((bf16[4,256,128]{2,1,0:T(8,128)(2,1)S(1)}, bf16[4,256,128]{2,1,0:T(8,128)(2,1)S(1)}, u32[]{:S(2)}, u32[]{:S(2)}) %collective-permute-start.10) | collective-permute-done | bytes 262176 | tf_op jit(solution)/shard_map/ppermute | solution.py:210
  73.1 2.5 %collective-permute-start.20 = (bf16[512,128]{1,0:T(8,128)(2,1)S(1)}, bf16[512,128]{1,0:T(8,128)(2,1)S(1)}, u32[]{:S(2)}, u32[]{:S(2)}) collective-permute-start(bf16[512,128]{1,0:T(8,128)(2,1)S(1)} %get-tuple-element.52), channel_id=1, source_target_pairs={{0,32},{16,48},{32,0},{48,16},{1,33},{17,49},{33,1},{49,17},{2,34}... | collective-permute-start | bytes 393224 | tf_op jit(solution)/shard_map/ppermute | solution.py:210
  80.4 16.6 %all-to-all-start = ((f32[256,1,128]{2,1,0:T(1,128)}), f32[256,1,128]{2,1,0:T(1,128)S(1)}, u32[]{:S(2)}, u32[]{:S(2)}) async-start(f32[256,1,128]{2,1,0:T(1,128)} %broadcast_in_dim.16), calls=%async_computation | async-start | bytes 262144 | tf_op jit(solution)/shard_map/all_to_all | solution.py:302
  98.5 11.2 %all-to-all-done = f32[256,1,128]{2,1,0:T(1,128)S(1)} async-done(((f32[256,1,128]{2,1,0:T(1,128)}), f32[256,1,128]{2,1,0:T(1,128)S(1)}, u32[]{:S(2)}, u32[]{:S(2)}) %all-to-all-start) | async-done | bytes 131104 | tf_op jit(solution)/shard_map/all_to_all | solution.py:302
  109.7 3.6 %all-to-all-start.1 = ((bf16[16,32,512]{2,1,0:T(8,128)(2,1)}), bf16[16,32,512]{2,1,0:T(8,128)(2,1)S(1)}, u32[]{:S(2)}, u32[]{:S(2)}) async-start(bf16[16,32,512]{2,1,0:T(8,128)(2,1)} %shard_map.116), calls=%async_computation.1 | async-start | bytes 1048576 | tf_op jit(solution)/shard_map/all_to_all | solution.py:287
  115.4 2.3 %collective-permute-start.22 = (bf16[128,512]{1,0:T(8,128)(2,1)S(1)}, bf16[128,512]{1,0:T(8,128)(2,1)S(1)}, u32[]{:S(2)}, u32[]{:S(2)}) collective-permute-start(bf16[128,512]{1,0:T(8,128)(2,1)S(1)} %convert_element_type.24), channel_id=1, source_target_pairs={{0,48},{16,0},{32,16},{48,32},{1,49},{17,1},{33,17},{49,33},{2,50}... | collective-permute-start | bytes 393224 | tf_op jit(solution)/shard_map/ppermute | solution.py:210
  119.2 12.9 %collective-permute-done.25.refs_3_ = f32[392,512]{1,0:T(8,128)S(1)} collective-permute-done((f32[392,512]{1,0:T(8,128)S(1)}, f32[392,512]{1,0:T(8,128)S(1)}, u32[]{:S(2)}, u32[]{:S(2)}) %collective-permute-start.25) | collective-permute-done | bytes 802848 | tf_op jit(solution)/shard_map/ppermute | solution.py:210
  132.8 2.5 %collective-permute-done.26.refs_4_ = f32[392,512]{1,0:T(8,128)S(1)} collective-permute-done((f32[392,512]{1,0:T(8,128)S(1)}, f32[392,512]{1,0:T(8,128)S(1)}, u32[]{:S(2)}, u32[]{:S(2)}) %collective-permute-start.26) | collective-permute-done | bytes 802848 | tf_op jit(solution)/shard_map/ppermute | solution.py:210
  135.3 18.1 %collective-permute-done.27.refs_5_ = f32[392,512]{1,0:T(8,128)S(1)} collective-permute-done((f32[392,512]{1,0:T(8,128)S(1)}, f32[392,512]{1,0:T(8,128)S(1)}, u32[]{:S(2)}, u32[]{:S(2)}) %collective-permute-start.27) | collective-permute-done | bytes 802848 | tf_op jit(solution)/shard_map/ppermute | solution.py:210
  155.4 3.2 %collective-permute-done.24.refs_2_ = bf16[128,512]{1,0:T(8,128)(2,1)S(1)} collective-permute-done((bf16[128,512]{1,0:T(8,128)(2,1)S(1)}, bf16[128,512]{1,0:T(8,128)(2,1)S(1)}, u32[]{:S(2)}, u32[]{:S(2)}) %collective-permute-start.24) | collective-permute-done | bytes 131104 | tf_op jit(solution)/shard_map/ppermute | solution.py:210
  160.0 21.2 %all_to_all.15 = bf16[16,32,512]{2,1,0:T(8,128)(2,1)S(1)} all-to-all(bf16[16,32,512]{2,1,0:T(8,128)(2,1)S(1)} %convolution_convert_fusion), channel_id=1, replica_groups=mesh['y_hi'=2,'core'=2,'x'=4,'y_lo'=2,'z'=8] {'y_lo','z'}, dimensions={0} | all-to-all | bytes 1048576 | tf_op jit(solution)/shard_map/all_to_all | solution.py:316
  (70 shorter events, 31.0 us)
Async XLA Ops:
  3.4 12.7 %collective-permute-start = (bf16[512,512]{1,0:T(8,128)(2,1)S(1)}, bf16[512,512]{1,0:T(8,128)(2,1)S(1)}, u32[]{:S(2)}, u32[]{:S(2)}) collective-permute-start(bf16[512,512]{1,0:T(8,128)(2,1)S(1)} %get-tuple-element.31), channel_id=1, source_target_pairs={{0,8},{8,0},{1,9},{9,1},{2,10},{10,2},{3,11},{11,3},{4,12},{12,4},... | collective-permute-start | bytes 1572872 | tf_op jit(solution)/shard_map/ppermute | solution.py:210
  6.7 20.6 %collective-permute-start.4 = (bf16[256,1024]{1,0:T(8,128)(2,1)S(1)}, bf16[256,1024]{1,0:T(8,128)(2,1)S(1)}, u32[]{:S(2)}, u32[]{:S(2)}) collective-permute-start(bf16[256,1024]{1,0:T(8,128)(2,1)S(1)} %get-tuple-element.35), channel_id=1, source_target_pairs={{0,8},{8,0},{1,9},{9,1},{2,10},{10,2},{3,11},{11,3},{4,12},{12,4},... | collective-permute-start | bytes 1572872 | tf_op jit(solution)/shard_map/ppermute | solution.py:210
  7.0 31.5 %collective-permute-start.3 = (bf16[256,1024]{1,0:T(8,128)(2,1)S(1)}, bf16[256,1024]{1,0:T(8,128)(2,1)S(1)}, u32[]{:S(2)}, u32[]{:S(2)}) collective-permute-start(bf16[256,1024]{1,0:T(8,128)(2,1)S(1)} %get-tuple-element.34), channel_id=1, source_target_pairs={{0,8},{8,0},{1,9},{9,1},{2,10},{10,2},{3,11},{11,3},{4,12},{12,4},... | collective-permute-start | bytes 1572872 | tf_op jit(solution)/shard_map/ppermute | solution.py:210
  17.0 10.3 %collective-permute-start.12 = (bf16[4,256,128]{2,1,0:T(8,128)(2,1)S(1)}, bf16[4,256,128]{2,1,0:T(8,128)(2,1)S(1)}, u32[]{:S(2)}, u32[]{:S(2)}) collective-permute-start(bf16[4,256,128]{2,1,0:T(8,128)(2,1)S(1)} %get-tuple-element.43), channel_id=1, source_target_pairs={{0,7},{1,0},{2,1},{3,2},{4,3},{5,4},{6,5},{7,6},{8,15},{9,8},{10,9... | collective-permute-start | bytes 786440 | tf_op jit(solution)/shard_map/ppermute | solution.py:210
  23.7 11.3 %collective-permute-start.5 = (bf16[4,256,128]{2,1,0:T(8,128)(2,1)S(1)}, bf16[4,256,128]{2,1,0:T(8,128)(2,1)S(1)}, u32[]{:S(2)}, u32[]{:S(2)}) collective-permute-start(bf16[4,256,128]{2,1,0:T(8,128)(2,1)S(1)} %get-tuple-element.36), channel_id=1, source_target_pairs={{0,1},{1,2},{2,3},{3,4},{4,5},{5,6},{6,7},{7,0},{8,9},{9,10},{10,1... | collective-permute-start | bytes 786440 | tf_op jit(solution)/shard_map/ppermute | solution.py:210
  23.7 29.2 %collective-permute-start.2 = (bf16[256,1024]{1,0:T(8,128)(2,1)S(1)}, bf16[256,1024]{1,0:T(8,128)(2,1)S(1)}, u32[]{:S(2)}, u32[]{:S(2)}) collective-permute-start(bf16[256,1024]{1,0:T(8,128)(2,1)S(1)} %get-tuple-element.33), channel_id=1, source_target_pairs={{0,8},{8,0},{1,9},{9,1},{2,10},{10,2},{3,11},{11,3},{4,12},{12,4},... | collective-permute-start | bytes 1572872 | tf_op jit(solution)/shard_map/ppermute | solution.py:210
  28.3 16.9 %collective-permute-start.13 = (bf16[4,256,128]{2,1,0:T(8,128)(2,1)S(1)}, bf16[4,256,128]{2,1,0:T(8,128)(2,1)S(1)}, u32[]{:S(2)}, u32[]{:S(2)}) collective-permute-start(bf16[4,256,128]{2,1,0:T(8,128)(2,1)S(1)} %get-tuple-element.44), channel_id=1, source_target_pairs={{0,1},{1,2},{2,3},{3,4},{4,5},{5,6},{6,7},{7,0},{8,9},{9,10},{10,1... | collective-permute-start | bytes 786440 | tf_op jit(solution)/shard_map/ppermute | solution.py:210
  31.1 14.1 %collective-permute-start.14 = (bf16[4,256,128]{2,1,0:T(8,128)(2,1)S(1)}, bf16[4,256,128]{2,1,0:T(8,128)(2,1)S(1)}, u32[]{:S(2)}, u32[]{:S(2)}) collective-permute-start(bf16[4,256,128]{2,1,0:T(8,128)(2,1)S(1)} %get-tuple-element.45), channel_id=1, source_target_pairs={{0,7},{1,0},{2,1},{3,2},{4,3},{5,4},{6,5},{7,6},{8,15},{9,8},{10,9... | collective-permute-start | bytes 786440 | tf_op jit(solution)/shard_map/ppermute | solution.py:210
  36.1 12.8 %collective-permute-start.6 = (bf16[4,256,128]{2,1,0:T(8,128)(2,1)S(1)}, bf16[4,256,128]{2,1,0:T(8,128)(2,1)S(1)}, u32[]{:S(2)}, u32[]{:S(2)}) collective-permute-start(bf16[4,256,128]{2,1,0:T(8,128)(2,1)S(1)} %get-tuple-element.37), channel_id=1, source_target_pairs={{0,1},{1,2},{2,3},{3,4},{4,5},{5,6},{6,7},{7,0},{8,9},{9,10},{10,1... | collective-permute-start | bytes 786440 | tf_op jit(solution)/shard_map/ppermute | solution.py:210
  38.5 10.4 %collective-permute-start.7 = (bf16[4,256,128]{2,1,0:T(8,128)(2,1)S(1)}, bf16[4,256,128]{2,1,0:T(8,128)(2,1)S(1)}, u32[]{:S(2)}, u32[]{:S(2)}) collective-permute-start(bf16[4,256,128]{2,1,0:T(8,128)(2,1)S(1)} %get-tuple-element.38), channel_id=1, source_target_pairs={{0,7},{1,0},{2,1},{3,2},{4,3},{5,4},{6,5},{7,6},{8,15},{9,8},{10,9... | collective-permute-start | bytes 786440 | tf_op jit(solution)/shard_map/ppermute | solution.py:210
  49.9 9.7 %collective-permute-start.8 = (bf16[4,256,128]{2,1,0:T(8,128)(2,1)S(1)}, bf16[4,256,128]{2,1,0:T(8,128)(2,1)S(1)}, u32[]{:S(2)}, u32[]{:S(2)}) collective-permute-start(bf16[4,256,128]{2,1,0:T(8,128)(2,1)S(1)} %get-tuple-element.39), channel_id=1, source_target_pairs={{0,1},{1,2},{2,3},{3,4},{4,5},{5,6},{6,7},{7,0},{8,9},{9,10},{10,1... | collective-permute-start | bytes 786440 | tf_op jit(solution)/shard_map/ppermute | solution.py:210
  50.0 10.0 %collective-permute-start.9 = (bf16[4,256,128]{2,1,0:T(8,128)(2,1)S(1)}, bf16[4,256,128]{2,1,0:T(8,128)(2,1)S(1)}, u32[]{:S(2)}, u32[]{:S(2)}) collective-permute-start(bf16[4,256,128]{2,1,0:T(8,128)(2,1)S(1)} %get-tuple-element.40), channel_id=1, source_target_pairs={{0,7},{1,0},{2,1},{3,2},{4,3},{5,4},{6,5},{7,6},{8,15},{9,8},{10,9... | collective-permute-start | bytes 786440 | tf_op jit(solution)/shard_map/ppermute | solution.py:210
  52.9 11.8 %collective-permute-start.1 = (bf16[256,512]{1,0:T(8,128)(2,1)S(1)}, bf16[256,512]{1,0:T(8,128)(2,1)S(1)}, u32[]{:S(2)}, u32[]{:S(2)}) collective-permute-start(bf16[256,512]{1,0:T(8,128)(2,1)S(1)} %get-tuple-element.32), channel_id=1, source_target_pairs={{0,8},{8,0},{1,9},{9,1},{2,10},{10,2},{3,11},{11,3},{4,12},{12,4},... | collective-permute-start | bytes 786440 | tf_op jit(solution)/shard_map/ppermute | solution.py:210
  56.0 9.7 %collective-permute-start.17 = (bf16[4,256,128]{2,1,0:T(8,128)(2,1)S(1)}, bf16[4,256,128]{2,1,0:T(8,128)(2,1)S(1)}, u32[]{:S(2)}, u32[]{:S(2)}) collective-permute-start(bf16[4,256,128]{2,1,0:T(8,128)(2,1)S(1)} %get-tuple-element.48), channel_id=1, source_target_pairs={{0,1},{1,2},{2,3},{3,4},{4,5},{5,6},{6,7},{7,0},{8,9},{9,10},{10,1... | collective-permute-start | bytes 786440 | tf_op jit(solution)/shard_map/ppermute | solution.py:210
  61.0 10.1 %collective-permute-start.10 = (bf16[4,256,128]{2,1,0:T(8,128)(2,1)S(1)}, bf16[4,256,128]{2,1,0:T(8,128)(2,1)S(1)}, u32[]{:S(2)}, u32[]{:S(2)}) collective-permute-start(bf16[4,256,128]{2,1,0:T(8,128)(2,1)S(1)} %get-tuple-element.41), channel_id=1, source_target_pairs={{0,1},{1,2},{2,3},{3,4},{4,5},{5,6},{6,7},{7,0},{8,9},{9,10},{10,1... | collective-permute-start | bytes 786440 | tf_op jit(solution)/shard_map/ppermute | solution.py:210
  61.1 10.0 %collective-permute-start.11 = (bf16[4,256,128]{2,1,0:T(8,128)(2,1)S(1)}, bf16[4,256,128]{2,1,0:T(8,128)(2,1)S(1)}, u32[]{:S(2)}, u32[]{:S(2)}) collective-permute-start(bf16[4,256,128]{2,1,0:T(8,128)(2,1)S(1)} %get-tuple-element.42), channel_id=1, source_target_pairs={{0,7},{1,0},{2,1},{3,2},{4,3},{5,4},{6,5},{7,6},{8,15},{9,8},{10,9... | collective-permute-start | bytes 786440 | tf_op jit(solution)/shard_map/ppermute | solution.py:210
  80.4 29.3 %all-to-all-start = ((f32[256,1,128]{2,1,0:T(1,128)}), f32[256,1,128]{2,1,0:T(1,128)S(1)}, u32[]{:S(2)}, u32[]{:S(2)}) async-start(f32[256,1,128]{2,1,0:T(1,128)} %broadcast_in_dim.16), calls=%async_computation | async-start | bytes 262144 | tf_op jit(solution)/shard_map/all_to_all | solution.py:302
  109.7 49.8 %all-to-all-start.1 = ((bf16[16,32,512]{2,1,0:T(8,128)(2,1)}), bf16[16,32,512]{2,1,0:T(8,128)(2,1)S(1)}, u32[]{:S(2)}, u32[]{:S(2)}) async-start(bf16[16,32,512]{2,1,0:T(8,128)(2,1)} %shard_map.116), calls=%async_computation.1 | async-start | bytes 1048576 | tf_op jit(solution)/shard_map/all_to_all | solution.py:287
  113.4 18.7 %collective-permute-start.25 = (f32[392,512]{1,0:T(8,128)S(1)}, f32[392,512]{1,0:T(8,128)S(1)}, u32[]{:S(2)}, u32[]{:S(2)}) collective-permute-start(f32[392,512]{1,0:T(8,128)S(1)} %maximum_maximum_fusion), channel_id=1, source_target_pairs={{0,48},{16,0},{32,16},{48,32},{1,49},{17,1},{33,17},{49,33},{2,50}... | collective-permute-start | bytes 2408456 | tf_op jit(solution)/shard_map/ppermute | solution.py:210
  114.7 20.6 %collective-permute-start.26 = (f32[392,512]{1,0:T(8,128)S(1)}, f32[392,512]{1,0:T(8,128)S(1)}, u32[]{:S(2)}, u32[]{:S(2)}) collective-permute-start(f32[392,512]{1,0:T(8,128)S(1)} %maximum_maximum_fusion), channel_id=1, source_target_pairs={{0,32},{16,48},{32,0},{48,16},{1,33},{17,49},{33,1},{49,17},{2,34}... | collective-permute-start | bytes 2408456 | tf_op jit(solution)/shard_map/ppermute | solution.py:210
  114.9 38.5 %collective-permute-start.27 = (f32[392,512]{1,0:T(8,128)S(1)}, f32[392,512]{1,0:T(8,128)S(1)}, u32[]{:S(2)}, u32[]{:S(2)}) collective-permute-start(f32[392,512]{1,0:T(8,128)S(1)} %maximum_maximum_fusion), channel_id=1, source_target_pairs={{0,16},{16,32},{32,48},{48,0},{1,17},{17,33},{33,49},{49,1},{2,18}... | collective-permute-start | bytes 2408456 | tf_op jit(solution)/shard_map/ppermute | solution.py:210
  115.4 38.0 %collective-permute-start.22 = (bf16[128,512]{1,0:T(8,128)(2,1)S(1)}, bf16[128,512]{1,0:T(8,128)(2,1)S(1)}, u32[]{:S(2)}, u32[]{:S(2)}) collective-permute-start(bf16[128,512]{1,0:T(8,128)(2,1)S(1)} %convert_element_type.24), channel_id=1, source_target_pairs={{0,48},{16,0},{32,16},{48,32},{1,49},{17,1},{33,17},{49,33},{2,50}... | collective-permute-start | bytes 393224 | tf_op jit(solution)/shard_map/ppermute | solution.py:210
  117.6 37.8 %collective-permute-start.23 = (bf16[128,512]{1,0:T(8,128)(2,1)S(1)}, bf16[128,512]{1,0:T(8,128)(2,1)S(1)}, u32[]{:S(2)}, u32[]{:S(2)}) collective-permute-start(bf16[128,512]{1,0:T(8,128)(2,1)S(1)} %convert_element_type.24), channel_id=1, source_target_pairs={{0,32},{16,48},{32,0},{48,16},{1,33},{17,49},{33,1},{49,17},{2,34}... | collective-permute-start | bytes 393224 | tf_op jit(solution)/shard_map/ppermute | solution.py:210
  132.2 26.4 %collective-permute-start.24 = (bf16[128,512]{1,0:T(8,128)(2,1)S(1)}, bf16[128,512]{1,0:T(8,128)(2,1)S(1)}, u32[]{:S(2)}, u32[]{:S(2)}) collective-permute-start(bf16[128,512]{1,0:T(8,128)(2,1)S(1)} %convert_element_type.24), channel_id=1, source_target_pairs={{0,16},{16,32},{32,48},{48,0},{1,17},{17,33},{33,49},{49,1},{2,18}... | collective-permute-start | bytes 393224 | tf_op jit(solution)/shard_map/ppermute | solution.py:210
  (11 other events, 224.9 us)
where the time goes:
time: 183 us; the launch traced here: 182 us
  waiting for transfers between devices  70.9 us (39%)
  starting transfers between devices  70.4 us (38%)
  blocking collectives  21.2 us (12%)
  Pallas kernels  14.5 us (8%)
  between operations  2.23 us (1%)
    ppermute x28, waiting for transfers between devices, shift(): return lax.ppermute(x, axis, [(i, (i + by) % n) for i in range(n)])  59.7 us
    ppermute x28, starting transfers between devices, shift(): return lax.ppermute(x, axis, [(i, (i + by) % n) for i in range(n)])  50.2 us
    all_to_all x1, blocking collectives, local(): parts = lax.all_to_all(partial, YZ, 0, 0, tiled=True)  21.2 us
    all_to_all x1, starting transfers between devices, local(): lax.all_to_all(part_sq, EVERY, 0, 0, tiled=True).reshape(COUNT, ROWS)  16.6 us
    pallas_call x13, Pallas kernels, on_core(): pl.pallas_call(kernel, in_specs=[SCALARS] * len(scalars) + [NEAR] * len(a...  12.5 us
    all_to_all x1, waiting for transfers between devices, local(): lax.all_to_all(part_sq, EVERY, 0, 0, tiled=True).reshape(COUNT, ROWS)  11.2 us
  transfers between devices with their start and end apart: 30, of which 14 were waited for; matrix products, arithmetic and copies ran while one was open for 0% of the time, Pallas kernels for 6%

commit v1 on v0

--- a/solution.py
+++ b/solution.py
@@ -134,12 +134,13 @@
 
 
 def gradient_kernel(scale, overflow, own, *refs):
-    gots, (grad, squares) = refs[: NX - 1], refs[NX - 1 :]
+    gots, (grad, rounded, squares) = refs[: NX - 1], refs[NX - 1 :]
     total = own[...]
     for got in gots:
         total += got[...].astype(f32)
     total = total.T * scale
     grad[...] = total
+    rounded[...] = total.astype(bf16)
     kept = jnp.where(overflow[0, 0] == 0, 1.0, 0.0)
     squares[...] = jnp.broadcast_to(jnp.sum(total * total) * kept, squares.shape)
 
@@ -241,6 +242,7 @@
 def sum_terms(where, tails, acts):
     tokens = acts.shape[0]
     two = lambda *shape: [pltpu.VMEM(shape, bf16)] * 2
+    loose = jax.ShapeDtypeStruct((NX, HALF, ROWS), bf16)
     z_pairs, give = first_terms(where, tails, acts)
     wide = [2 * Z_WIDE] * (NZ // 2 - 1) + [Z_WIDE]
     gives = on_core(pack_kernel, [where], [acts], [pltpu.VMEM((tokens, w), bf16) for w in wide])
@@ -256,7 +258,7 @@
                 functools.partial(later_z_kernel, s, half, ways),
                 [where],
                 [z_pairs, acts, joined, parts[s - 1], *[came[half, way] for way in ways]],
-                two(NX, HALF, ROWS),
+                two(NX, HALF, ROWS) if s + 1 < NZ // 2 else [loose] * 2,
             )
             gots[half, 0] = shift(up, "z", NZ, 1)
             gots[half, 1] = shift(down, "z", NZ, -1)
@@ -292,15 +294,19 @@
     states = [shift(state, "x", NX, -r) for r in range(1, NX)]
 
     own, gots = sum_terms(where, tails, acts)
-    gradient, part_sq = on_core(
+    gradient, rounded, part_sq = on_core(
         functools.partial(gradient_kernel, 1.0 / (tok_dev * NX * NY * NZ)),
         [overflow],
         [own, *gots],
-        [pltpu.VMEM((ROWS, COLS), f32), pltpu.VMEM((1, ROWS), f32)],
-    )
-    part_sq = jnp.broadcast_to(part_sq[None], (COUNT, 1, ROWS))
+        [
+            pltpu.VMEM((ROWS, COLS), f32),
+            jax.ShapeDtypeStruct((ROWS, COLS), bf16),
+            jax.ShapeDtypeStruct((COUNT, ROWS), f32),
+        ],
+    )
+    gots = [shift(rounded, "x", NX, -r) for r in range(1, NX)]
+    part_sq = part_sq.reshape(COUNT, 1, ROWS)
     squares = lax.all_to_all(part_sq, EVERY, 0, 0, tiled=True).reshape(COUNT, ROWS)
-    gots = [shift(gradient.astype(bf16), "x", NX, -r) for r in range(1, NX)]
     updated, along_x = on_core(
         adam_kernel,
         [overflow, clip_on],

time: 183 us -> 183 us (level)
  no operation moved by 1% of the time
where the time goes in v1:
time: 183 us; the launch traced here: 182 us
  waiting for transfers between devices  71 us (39%)
  starting transfers between devices  70.3 us (38%)
  blocking collectives  21.2 us (12%)
  Pallas kernels  15.2 us (8%)
  between operations  2.22 us (1%)
    ppermute x28, waiting for transfers between devices, shift(): return lax.ppermute(x, axis, [(i, (i + by) % n) for i in range(n)])  59.8 us
    ppermute x28, starting transfers between devices, shift(): return lax.ppermute(x, axis, [(i, (i + by) % n) for i in range(n)])  50.1 us
    all_to_all x1, blocking collectives, local(): parts = lax.all_to_all(partial, YZ, 0, 0, tiled=True)  21.2 us
    all_to_all x1, starting transfers between devices, local(): lax.all_to_all(part_sq, EVERY, 0, 0, tiled=True).reshape(COUNT, ROWS)  16.6 us
    pallas_call x13, Pallas kernels, on_core(): pl.pallas_call(kernel, in_specs=[SCALARS] * len(scalars) + [NEAR] * len(a...  13.2 us
    all_to_all x1, waiting for transfers between devices, local(): lax.all_to_all(part_sq, EVERY, 0, 0, tiled=True).reshape(COUNT, ROWS)  11.2 us
  transfers between devices with their start and end apart: 30, of which 14 were waited for; matrix products, arithmetic and copies ran while one was open for 0% of the time, Pallas kernels for 6%

profile of v1, /device:TPU:1, one launch (start us, length us, event | category | flops | bytes accessed | tf_op | source)
XLA Modules:
  0.0 181.8 jit_solution(15019041359187395100)
XLA Ops:
  1.4 2.0 %work_first.1 = (bf16[512,256]{1,0:T(8,128)(2,1)S(1)}, bf16[512,512]{1,0:T(8,128)(2,1)S(1)}) custom-call(s32[7]{0:T(128)S(1)} %pad_add_fusion.where, bf16[256,512]{1,0:T(8,128)(2,1)} %bitcast.43, bf16[256,8192]{1,0:T(8,128)(2,1)} %bitcast.22, bf16[256,8192]{1,0:T(8,128)(2,1)} %bitcast.23, bf16[256,8192]{1,0:T(8,128)(2,1)} %bitcast.24, bf16[256,8192]{1,0:T(8,128)(2,1)} %bitcast.25), custom_call_target="tpu_custom_call" | custom-call | tf_op jit(solution)/shard_map/work_first/pallas_call | solution.py:226
  3.4 2.2 %collective-permute-start = (bf16[512,512]{1,0:T(8,128)(2,1)S(1)}, bf16[512,512]{1,0:T(8,128)(2,1)S(1)}, u32[]{:S(2)}, u32[]{:S(2)}) collective-permute-start(bf16[512,512]{1,0:T(8,128)(2,1)S(1)} %get-tuple-element.32), channel_id=1, source_target_pairs={{0,8},{8,0},{1,9},{9,1},{2,10},{10,2},{3,11},{11,3},{4,12},{12,4},... | collective-permute-start | bytes 1572872 | tf_op jit(solution)/shard_map/ppermute | solution.py:211
  8.2 7.8 %collective-permute-done.joined = bf16[512,512]{1,0:T(8,128)(2,1)S(1)} collective-permute-done((bf16[512,512]{1,0:T(8,128)(2,1)S(1)}, bf16[512,512]{1,0:T(8,128)(2,1)S(1)}, u32[]{:S(2)}, u32[]{:S(2)}) %collective-permute-start) | collective-permute-done | bytes 524320 | tf_op jit(solution)/shard_map/ppermute | solution.py:211
  17.0 6.7 %collective-permute-start.12 = (bf16[4,256,128]{2,1,0:T(8,128)(2,1)S(1)}, bf16[4,256,128]{2,1,0:T(8,128)(2,1)S(1)}, u32[]{:S(2)}, u32[]{:S(2)}) collective-permute-start(bf16[4,256,128]{2,1,0:T(8,128)(2,1)S(1)} %get-tuple-element.44), channel_id=1, source_target_pairs={{0,7},{1,0},{2,1},{3,2},{4,3},{5,4},{6,5},{7,6},{8,15},{9,8},{10,9... | collective-permute-start | bytes 786440 | tf_op jit(solution)/shard_map/ppermute | solution.py:211
  25.0 2.3 %collective-permute-done.4.part = bf16[256,1024]{1,0:T(8,128)(2,1)S(1)} collective-permute-done((bf16[256,1024]{1,0:T(8,128)(2,1)S(1)}, bf16[256,1024]{1,0:T(8,128)(2,1)S(1)}, u32[]{:S(2)}, u32[]{:S(2)}) %collective-permute-start.4) | collective-permute-done | bytes 524320 | tf_op jit(solution)/shard_map/ppermute | solution.py:211
  28.3 2.8 %collective-permute-start.13 = (bf16[4,256,128]{2,1,0:T(8,128)(2,1)S(1)}, bf16[4,256,128]{2,1,0:T(8,128)(2,1)S(1)}, u32[]{:S(2)}, u32[]{:S(2)}) collective-permute-start(bf16[4,256,128]{2,1,0:T(8,128)(2,1)S(1)} %get-tuple-element.45), channel_id=1, source_target_pairs={{0,1},{1,2},{2,3},{3,4},{4,5},{5,6},{6,7},{7,0},{8,9},{9,10},{10,1... | collective-permute-start | bytes 786440 | tf_op jit(solution)/shard_map/ppermute | solution.py:211
  31.1 4.0 %collective-permute-start.14 = (bf16[4,256,128]{2,1,0:T(8,128)(2,1)S(1)}, bf16[4,256,128]{2,1,0:T(8,128)(2,1)S(1)}, u32[]{:S(2)}, u32[]{:S(2)}) collective-permute-start(bf16[4,256,128]{2,1,0:T(8,128)(2,1)S(1)} %get-tuple-element.46), channel_id=1, source_target_pairs={{0,7},{1,0},{2,1},{3,2},{4,3},{5,4},{6,5},{7,6},{8,15},{9,8},{10,9... | collective-permute-start | bytes 786440 | tf_op jit(solution)/shard_map/ppermute | solution.py:211
  36.2 2.3 %collective-permute-done.3.part = bf16[256,1024]{1,0:T(8,128)(2,1)S(1)} collective-permute-done((bf16[256,1024]{1,0:T(8,128)(2,1)S(1)}, bf16[256,1024]{1,0:T(8,128)(2,1)S(1)}, u32[]{:S(2)}, u32[]{:S(2)}) %collective-permute-start.3) | collective-permute-done | bytes 524320 | tf_op jit(solution)/shard_map/ppermute | solution.py:211
  38.5 6.6 %collective-permute-start.7 = (bf16[4,256,128]{2,1,0:T(8,128)(2,1)S(1)}, bf16[4,256,128]{2,1,0:T(8,128)(2,1)S(1)}, u32[]{:S(2)}, u32[]{:S(2)}) collective-permute-start(bf16[4,256,128]{2,1,0:T(8,128)(2,1)S(1)} %get-tuple-element.39), channel_id=1, source_target_pairs={{0,7},{1,0},{2,1},{3,2},{4,3},{5,4},{6,5},{7,6},{8,15},{9,8},{10,9... | collective-permute-start | bytes 786440 | tf_op jit(solution)/shard_map/ppermute | solution.py:211
  46.2 2.7 %collective-permute-start.16 = (bf16[4,256,128]{2,1,0:T(8,128)(2,1)S(1)}, bf16[4,256,128]{2,1,0:T(8,128)(2,1)S(1)}, u32[]{:S(2)}, u32[]{:S(2)}) collective-permute-start(bf16[4,256,128]{2,1,0:T(8,128)(2,1)S(1)} %get-tuple-element.48), channel_id=1, source_target_pairs={{0,7},{1,0},{2,1},{3,2},{4,3},{5,4},{6,5},{7,6},{8,15},{9,8},{10,9... | collective-permute-start | bytes 786440 | tf_op jit(solution)/shard_map/ppermute | solution.py:211
  50.0 2.9 %collective-permute-start.9 = (bf16[4,256,128]{2,1,0:T(8,128)(2,1)S(1)}, bf16[4,256,128]{2,1,0:T(8,128)(2,1)S(1)}, u32[]{:S(2)}, u32[]{:S(2)}) collective-permute-start(bf16[4,256,128]{2,1,0:T(8,128)(2,1)S(1)} %get-tuple-element.41), channel_id=1, source_target_pairs={{0,7},{1,0},{2,1},{3,2},{4,3},{5,4},{6,5},{7,6},{8,15},{9,8},{10,9... | collective-permute-start | bytes 786440 | tf_op jit(solution)/shard_map/ppermute | solution.py:211
  56.1 3.5 %collective-permute-start.18 = (bf16[4,256,128]{2,1,0:T(8,128)(2,1)S(1)}, bf16[4,256,128]{2,1,0:T(8,128)(2,1)S(1)}, u32[]{:S(2)}, u32[]{:S(2)}) collective-permute-start(bf16[4,256,128]{2,1,0:T(8,128)(2,1)S(1)} %get-tuple-element.50), channel_id=1, source_target_pairs={{0,7},{1,0},{2,1},{3,2},{4,3},{5,4},{6,5},{7,6},{8,15},{9,8},{10,9... | collective-permute-start | bytes 786440 | tf_op jit(solution)/shard_map/ppermute | solution.py:211
  61.2 3.6 %collective-permute-start.11 = (bf16[4,256,128]{2,1,0:T(8,128)(2,1)S(1)}, bf16[4,256,128]{2,1,0:T(8,128)(2,1)S(1)}, u32[]{:S(2)}, u32[]{:S(2)}) collective-permute-start(bf16[4,256,128]{2,1,0:T(8,128)(2,1)S(1)} %get-tuple-element.43), channel_id=1, source_target_pairs={{0,7},{1,0},{2,1},{3,2},{4,3},{5,4},{6,5},{7,6},{8,15},{9,8},{10,9... | collective-permute-start | bytes 786440 | tf_op jit(solution)/shard_map/ppermute | solution.py:211
  65.8 5.3 %collective-permute-done.10.refs_0_ = bf16[4,256,128]{2,1,0:T(8,128)(2,1)S(1)} collective-permute-done((bf16[4,256,128]{2,1,0:T(8,128)(2,1)S(1)}, bf16[4,256,128]{2,1,0:T(8,128)(2,1)S(1)}, u32[]{:S(2)}, u32[]{:S(2)}) %collective-permute-start.10) | collective-permute-done | bytes 262176 | tf_op jit(solution)/shard_map/ppermute | solution.py:211
  73.1 2.5 %collective-permute-start.20 = (bf16[512,128]{1,0:T(8,128)(2,1)S(1)}, bf16[512,128]{1,0:T(8,128)(2,1)S(1)}, u32[]{:S(2)}, u32[]{:S(2)}) collective-permute-start(bf16[512,128]{1,0:T(8,128)(2,1)S(1)} %get-tuple-element.53), channel_id=1, source_target_pairs={{0,32},{16,48},{32,0},{48,16},{1,33},{17,49},{33,1},{49,17},{2,34}... | collective-permute-start | bytes 393224 | tf_op jit(solution)/shard_map/ppermute | solution.py:211
  80.3 16.6 %all-to-all-start = ((f32[256,1,128]{2,1,0:T(1,128)}), f32[256,1,128]{2,1,0:T(1,128)S(1)}, u32[]{:S(2)}, u32[]{:S(2)}) async-start(f32[256,1,128]{2,1,0:T(1,128)} %bitcast.7), calls=%async_computation | async-start | bytes 262144 | tf_op jit(solution)/shard_map/all_to_all | solution.py:309
  98.5 11.2 %all-to-all-done = f32[256,1,128]{2,1,0:T(1,128)S(1)} async-done(((f32[256,1,128]{2,1,0:T(1,128)}), f32[256,1,128]{2,1,0:T(1,128)S(1)}, u32[]{:S(2)}, u32[]{:S(2)}) %all-to-all-start) | async-done | bytes 131104 | tf_op jit(solution)/shard_map/all_to_all | solution.py:309
  109.7 3.6 %all-to-all-start.1 = ((bf16[16,32,512]{2,1,0:T(8,128)(2,1)}), bf16[16,32,512]{2,1,0:T(8,128)(2,1)S(1)}, u32[]{:S(2)}, u32[]{:S(2)}) async-start(bf16[16,32,512]{2,1,0:T(8,128)(2,1)} %shard_map.116), calls=%async_computation.1 | async-start | bytes 1048576 | tf_op jit(solution)/shard_map/all_to_all | solution.py:289
  115.3 2.2 %collective-permute-start.22 = (bf16[128,512]{1,0:T(8,128)(2,1)S(1)}, bf16[128,512]{1,0:T(8,128)(2,1)S(1)}, u32[]{:S(2)}, u32[]{:S(2)}) collective-permute-start(bf16[128,512]{1,0:T(8,128)(2,1)S(1)} %get-tuple-element.57), channel_id=1, source_target_pairs={{0,48},{16,0},{32,16},{48,32},{1,49},{17,1},{33,17},{49,33},{2,50}... | collective-permute-start | bytes 393224 | tf_op jit(solution)/shard_map/ppermute | solution.py:211
  119.1 13.0 %collective-permute-done.25.refs_3_ = f32[392,512]{1,0:T(8,128)S(1)} collective-permute-done((f32[392,512]{1,0:T(8,128)S(1)}, f32[392,512]{1,0:T(8,128)S(1)}, u32[]{:S(2)}, u32[]{:S(2)}) %collective-permute-start.25) | collective-permute-done | bytes 802848 | tf_op jit(solution)/shard_map/ppermute | solution.py:211
  132.8 2.5 %collective-permute-done.26.refs_4_ = f32[392,512]{1,0:T(8,128)S(1)} collective-permute-done((f32[392,512]{1,0:T(8,128)S(1)}, f32[392,512]{1,0:T(8,128)S(1)}, u32[]{:S(2)}, u32[]{:S(2)}) %collective-permute-start.26) | collective-permute-done | bytes 802848 | tf_op jit(solution)/shard_map/ppermute | solution.py:211
  135.3 18.1 %collective-permute-done.27.refs_5_ = f32[392,512]{1,0:T(8,128)S(1)} collective-permute-done((f32[392,512]{1,0:T(8,128)S(1)}, f32[392,512]{1,0:T(8,128)S(1)}, u32[]{:S(2)}, u32[]{:S(2)}) %collective-permute-start.27) | collective-permute-done | bytes 802848 | tf_op jit(solution)/shard_map/ppermute | solution.py:211
  155.4 3.2 %collective-permute-done.24.refs_2_ = bf16[128,512]{1,0:T(8,128)(2,1)S(1)} collective-permute-done((bf16[128,512]{1,0:T(8,128)(2,1)S(1)}, bf16[128,512]{1,0:T(8,128)(2,1)S(1)}, u32[]{:S(2)}, u32[]{:S(2)}) %collective-permute-start.24) | collective-permute-done | bytes 131104 | tf_op jit(solution)/shard_map/ppermute | solution.py:211
  160.0 21.2 %all_to_all.15 = bf16[16,32,512]{2,1,0:T(8,128)(2,1)S(1)} all-to-all(bf16[16,32,512]{2,1,0:T(8,128)(2,1)S(1)} %convolution_convert_fusion), channel_id=1, replica_groups=mesh['y_hi'=2,'core'=2,'x'=4,'y_lo'=2,'z'=8] {'y_lo','z'}, dimensions={0} | all-to-all | bytes 1048576 | tf_op jit(solution)/shard_map/all_to_all | solution.py:322
  (68 shorter events, 30.9 us)
Async XLA Ops:
  3.4 12.7 %collective-permute-start = (bf16[512,512]{1,0:T(8,128)(2,1)S(1)}, bf16[512,512]{1,0:T(8,128)(2,1)S(1)}, u32[]{:S(2)}, u32[]{:S(2)}) collective-permute-start(bf16[512,512]{1,0:T(8,128)(2,1)S(1)} %get-tuple-element.32), channel_id=1, source_target_pairs={{0,8},{8,0},{1,9},{9,1},{2,10},{10,2},{3,11},{11,3},{4,12},{12,4},... | collective-permute-start | bytes 1572872 | tf_op jit(solution)/shard_map/ppermute | solution.py:211
  6.7 20.6 %collective-permute-start.4 = (bf16[256,1024]{1,0:T(8,128)(2,1)S(1)}, bf16[256,1024]{1,0:T(8,128)(2,1)S(1)}, u32[]{:S(2)}, u32[]{:S(2)}) collective-permute-start(bf16[256,1024]{1,0:T(8,128)(2,1)S(1)} %get-tuple-element.36), channel_id=1, source_target_pairs={{0,8},{8,0},{1,9},{9,1},{2,10},{10,2},{3,11},{11,3},{4,12},{12,4},... | collective-permute-start | bytes 1572872 | tf_op jit(solution)/shard_map/ppermute | solution.py:211
  7.0 31.5 %collective-permute-start.3 = (bf16[256,1024]{1,0:T(8,128)(2,1)S(1)}, bf16[256,1024]{1,0:T(8,128)(2,1)S(1)}, u32[]{:S(2)}, u32[]{:S(2)}) collective-permute-start(bf16[256,1024]{1,0:T(8,128)(2,1)S(1)} %get-tuple-element.35), channel_id=1, source_target_pairs={{0,8},{8,0},{1,9},{9,1},{2,10},{10,2},{3,11},{11,3},{4,12},{12,4},... | collective-permute-start | bytes 1572872 | tf_op jit(solution)/shard_map/ppermute | solution.py:211
  17.0 10.3 %collective-permute-start.12 = (bf16[4,256,128]{2,1,0:T(8,128)(2,1)S(1)}, bf16[4,256,128]{2,1,0:T(8,128)(2,1)S(1)}, u32[]{:S(2)}, u32[]{:S(2)}) collective-permute-start(bf16[4,256,128]{2,1,0:T(8,128)(2,1)S(1)} %get-tuple-element.44), channel_id=1, source_target_pairs={{0,7},{1,0},{2,1},{3,2},{4,3},{5,4},{6,5},{7,6},{8,15},{9,8},{10,9... | collective-permute-start | bytes 786440 | tf_op jit(solution)/shard_map/ppermute | solution.py:211
  23.7 11.3 %collective-permute-start.5 = (bf16[4,256,128]{2,1,0:T(8,128)(2,1)S(1)}, bf16[4,256,128]{2,1,0:T(8,128)(2,1)S(1)}, u32[]{:S(2)}, u32[]{:S(2)}) collective-permute-start(bf16[4,256,128]{2,1,0:T(8,128)(2,1)S(1)} %get-tuple-element.37), channel_id=1, source_target_pairs={{0,1},{1,2},{2,3},{3,4},{4,5},{5,6},{6,7},{7,0},{8,9},{9,10},{10,1... | collective-permute-start | bytes 786440 | tf_op jit(solution)/shard_map/ppermute | solution.py:211
  23.7 29.2 %collective-permute-start.2 = (bf16[256,1024]{1,0:T(8,128)(2,1)S(1)}, bf16[256,1024]{1,0:T(8,128)(2,1)S(1)}, u32[]{:S(2)}, u32[]{:S(2)}) collective-permute-start(bf16[256,1024]{1,0:T(8,128)(2,1)S(1)} %get-tuple-element.34), channel_id=1, source_target_pairs={{0,8},{8,0},{1,9},{9,1},{2,10},{10,2},{3,11},{11,3},{4,12},{12,4},... | collective-permute-start | bytes 1572872 | tf_op jit(solution)/shard_map/ppermute | solution.py:211
  28.3 16.9 %collective-permute-start.13 = (bf16[4,256,128]{2,1,0:T(8,128)(2,1)S(1)}, bf16[4,256,128]{2,1,0:T(8,128)(2,1)S(1)}, u32[]{:S(2)}, u32[]{:S(2)}) collective-permute-start(bf16[4,256,128]{2,1,0:T(8,128)(2,1)S(1)} %get-tuple-element.45), channel_id=1, source_target_pairs={{0,1},{1,2},{2,3},{3,4},{4,5},{5,6},{6,7},{7,0},{8,9},{9,10},{10,1... | collective-permute-start | bytes 786440 | tf_op jit(solution)/shard_map/ppermute | solution.py:211
  31.1 14.1 %collective-permute-start.14 = (bf16[4,256,128]{2,1,0:T(8,128)(2,1)S(1)}, bf16[4,256,128]{2,1,0:T(8,128)(2,1)S(1)}, u32[]{:S(2)}, u32[]{:S(2)}) collective-permute-start(bf16[4,256,128]{2,1,0:T(8,128)(2,1)S(1)} %get-tuple-element.46), channel_id=1, source_target_pairs={{0,7},{1,0},{2,1},{3,2},{4,3},{5,4},{6,5},{7,6},{8,15},{9,8},{10,9... | collective-permute-start | bytes 786440 | tf_op jit(solution)/shard_map/ppermute | solution.py:211
  36.1 12.8 %collective-permute-start.6 = (bf16[4,256,128]{2,1,0:T(8,128)(2,1)S(1)}, bf16[4,256,128]{2,1,0:T(8,128)(2,1)S(1)}, u32[]{:S(2)}, u32[]{:S(2)}) collective-permute-start(bf16[4,256,128]{2,1,0:T(8,128)(2,1)S(1)} %get-tuple-element.38), channel_id=1, source_target_pairs={{0,1},{1,2},{2,3},{3,4},{4,5},{5,6},{6,7},{7,0},{8,9},{9,10},{10,1... | collective-permute-start | bytes 786440 | tf_op jit(solution)/shard_map/ppermute | solution.py:211
  38.5 10.4 %collective-permute-start.7 = (bf16[4,256,128]{2,1,0:T(8,128)(2,1)S(1)}, bf16[4,256,128]{2,1,0:T(8,128)(2,1)S(1)}, u32[]{:S(2)}, u32[]{:S(2)}) collective-permute-start(bf16[4,256,128]{2,1,0:T(8,128)(2,1)S(1)} %get-tuple-element.39), channel_id=1, source_target_pairs={{0,7},{1,0},{2,1},{3,2},{4,3},{5,4},{6,5},{7,6},{8,15},{9,8},{10,9... | collective-permute-start | bytes 786440 | tf_op jit(solution)/shard_map/ppermute | solution.py:211
  49.9 9.7 %collective-permute-start.8 = (bf16[4,256,128]{2,1,0:T(8,128)(2,1)S(1)}, bf16[4,256,128]{2,1,0:T(8,128)(2,1)S(1)}, u32[]{:S(2)}, u32[]{:S(2)}) collective-permute-start(bf16[4,256,128]{2,1,0:T(8,128)(2,1)S(1)} %get-tuple-element.40), channel_id=1, source_target_pairs={{0,1},{1,2},{2,3},{3,4},{4,5},{5,6},{6,7},{7,0},{8,9},{9,10},{10,1... | collective-permute-start | bytes 786440 | tf_op jit(solution)/shard_map/ppermute | solution.py:211
  50.0 10.0 %collective-permute-start.9 = (bf16[4,256,128]{2,1,0:T(8,128)(2,1)S(1)}, bf16[4,256,128]{2,1,0:T(8,128)(2,1)S(1)}, u32[]{:S(2)}, u32[]{:S(2)}) collective-permute-start(bf16[4,256,128]{2,1,0:T(8,128)(2,1)S(1)} %get-tuple-element.41), channel_id=1, source_target_pairs={{0,7},{1,0},{2,1},{3,2},{4,3},{5,4},{6,5},{7,6},{8,15},{9,8},{10,9... | collective-permute-start | bytes 786440 | tf_op jit(solution)/shard_map/ppermute | solution.py:211
  52.9 11.8 %collective-permute-start.1 = (bf16[256,512]{1,0:T(8,128)(2,1)S(1)}, bf16[256,512]{1,0:T(8,128)(2,1)S(1)}, u32[]{:S(2)}, u32[]{:S(2)}) collective-permute-start(bf16[256,512]{1,0:T(8,128)(2,1)S(1)} %get-tuple-element.33), channel_id=1, source_target_pairs={{0,8},{8,0},{1,9},{9,1},{2,10},{10,2},{3,11},{11,3},{4,12},{12,4},... | collective-permute-start | bytes 786440 | tf_op jit(solution)/shard_map/ppermute | solution.py:211
  56.0 9.7 %collective-permute-start.17 = (bf16[4,256,128]{2,1,0:T(8,128)(2,1)S(1)}, bf16[4,256,128]{2,1,0:T(8,128)(2,1)S(1)}, u32[]{:S(2)}, u32[]{:S(2)}) collective-permute-start(bf16[4,256,128]{2,1,0:T(8,128)(2,1)S(1)} %get-tuple-element.49), channel_id=1, source_target_pairs={{0,1},{1,2},{2,3},{3,4},{4,5},{5,6},{6,7},{7,0},{8,9},{9,10},{10,1... | collective-permute-start | bytes 786440 | tf_op jit(solution)/shard_map/ppermute | solution.py:211
  61.0 10.1 %collective-permute-start.10 = (bf16[4,256,128]{2,1,0:T(8,128)(2,1)S(1)}, bf16[4,256,128]{2,1,0:T(8,128)(2,1)S(1)}, u32[]{:S(2)}, u32[]{:S(2)}) collective-permute-start(bf16[4,256,128]{2,1,0:T(8,128)(2,1)S(1)} %get-tuple-element.42), channel_id=1, source_target_pairs={{0,1},{1,2},{2,3},{3,4},{4,5},{5,6},{6,7},{7,0},{8,9},{9,10},{10,1... | collective-permute-start | bytes 786440 | tf_op jit(solution)/shard_map/ppermute | solution.py:211
  61.2 10.0 %collective-permute-start.11 = (bf16[4,256,128]{2,1,0:T(8,128)(2,1)S(1)}, bf16[4,256,128]{2,1,0:T(8,128)(2,1)S(1)}, u32[]{:S(2)}, u32[]{:S(2)}) collective-permute-start(bf16[4,256,128]{2,1,0:T(8,128)(2,1)S(1)} %get-tuple-element.43), channel_id=1, source_target_pairs={{0,7},{1,0},{2,1},{3,2},{4,3},{5,4},{6,5},{7,6},{8,15},{9,8},{10,9... | collective-permute-start | bytes 786440 | tf_op jit(solution)/shard_map/ppermute | solution.py:211
  80.3 29.3 %all-to-all-start = ((f32[256,1,128]{2,1,0:T(1,128)}), f32[256,1,128]{2,1,0:T(1,128)S(1)}, u32[]{:S(2)}, u32[]{:S(2)}) async-start(f32[256,1,128]{2,1,0:T(1,128)} %bitcast.7), calls=%async_computation | async-start | bytes 262144 | tf_op jit(solution)/shard_map/all_to_all | solution.py:309
  109.7 49.8 %all-to-all-start.1 = ((bf16[16,32,512]{2,1,0:T(8,128)(2,1)}), bf16[16,32,512]{2,1,0:T(8,128)(2,1)S(1)}, u32[]{:S(2)}, u32[]{:S(2)}) async-start(bf16[16,32,512]{2,1,0:T(8,128)(2,1)} %shard_map.116), calls=%async_computation.1 | async-start | bytes 1048576 | tf_op jit(solution)/shard_map/all_to_all | solution.py:289
  113.4 18.7 %collective-permute-start.25 = (f32[392,512]{1,0:T(8,128)S(1)}, f32[392,512]{1,0:T(8,128)S(1)}, u32[]{:S(2)}, u32[]{:S(2)}) collective-permute-start(f32[392,512]{1,0:T(8,128)S(1)} %maximum_maximum_fusion), channel_id=1, source_target_pairs={{0,48},{16,0},{32,16},{48,32},{1,49},{17,1},{33,17},{49,33},{2,50}... | collective-permute-start | bytes 2408456 | tf_op jit(solution)/shard_map/ppermute | solution.py:211
  114.7 20.6 %collective-permute-start.26 = (f32[392,512]{1,0:T(8,128)S(1)}, f32[392,512]{1,0:T(8,128)S(1)}, u32[]{:S(2)}, u32[]{:S(2)}) collective-permute-start(f32[392,512]{1,0:T(8,128)S(1)} %maximum_maximum_fusion), channel_id=1, source_target_pairs={{0,32},{16,48},{32,0},{48,16},{1,33},{17,49},{33,1},{49,17},{2,34}... | collective-permute-start | bytes 2408456 | tf_op jit(solution)/shard_map/ppermute | solution.py:211
  114.8 38.5 %collective-permute-start.27 = (f32[392,512]{1,0:T(8,128)S(1)}, f32[392,512]{1,0:T(8,128)S(1)}, u32[]{:S(2)}, u32[]{:S(2)}) collective-permute-start(f32[392,512]{1,0:T(8,128)S(1)} %maximum_maximum_fusion), channel_id=1, source_target_pairs={{0,16},{16,32},{32,48},{48,0},{1,17},{17,33},{33,49},{49,1},{2,18}... | collective-permute-start | bytes 2408456 | tf_op jit(solution)/shard_map/ppermute | solution.py:211
  115.3 38.0 %collective-permute-start.22 = (bf16[128,512]{1,0:T(8,128)(2,1)S(1)}, bf16[128,512]{1,0:T(8,128)(2,1)S(1)}, u32[]{:S(2)}, u32[]{:S(2)}) collective-permute-start(bf16[128,512]{1,0:T(8,128)(2,1)S(1)} %get-tuple-element.57), channel_id=1, source_target_pairs={{0,48},{16,0},{32,16},{48,32},{1,49},{17,1},{33,17},{49,33},{2,50}... | collective-permute-start | bytes 393224 | tf_op jit(solution)/shard_map/ppermute | solution.py:211
  117.5 37.8 %collective-permute-start.23 = (bf16[128,512]{1,0:T(8,128)(2,1)S(1)}, bf16[128,512]{1,0:T(8,128)(2,1)S(1)}, u32[]{:S(2)}, u32[]{:S(2)}) collective-permute-start(bf16[128,512]{1,0:T(8,128)(2,1)S(1)} %get-tuple-element.57), channel_id=1, source_target_pairs={{0,32},{16,48},{32,0},{48,16},{1,33},{17,49},{33,1},{49,17},{2,34}... | collective-permute-start | bytes 393224 | tf_op jit(solution)/shard_map/ppermute | solution.py:211
  132.1 26.4 %collective-permute-start.24 = (bf16[128,512]{1,0:T(8,128)(2,1)S(1)}, bf16[128,512]{1,0:T(8,128)(2,1)S(1)}, u32[]{:S(2)}, u32[]{:S(2)}) collective-permute-start(bf16[128,512]{1,0:T(8,128)(2,1)S(1)} %get-tuple-element.57), channel_id=1, source_target_pairs={{0,16},{16,32},{32,48},{48,0},{1,17},{17,33},{33,49},{49,1},{2,18}... | collective-permute-start | bytes 393224 | tf_op jit(solution)/shard_map/ppermute | solution.py:211
  (11 other events, 238.6 us)
